TPU v7x, 128 devices: a whole 4x4x4 slice. The times are simulated.
128 devices in a mesh: row: 16 (over z_lo, x, core), col: 8 (over y, z_hi).
Axes of the slice: x: 4, y: 4, z: 4 (z_hi: 2, z_lo: 2; z = z_hi * 2 + z_lo), core: 2. Of those that a mesh axis runs over, the one named last changes fastest.
Arguments:
- amplitudes: bfloat16 [7168, 7168], P('row', 'col'), as said below
- integrals: bfloat16 [7168, 7168], P('row', 'col'), as said below
- occ_energy: float32 [80], replicated, may hold values from -2 to -0.5
- vir_energy: float32 [1000], replicated, may hold values from 0.5 to 4
- pair_occ: int32 [7168], replicated, may hold values from 0 to 79, as said below
- pair_vir: int32 [7168], replicated, may hold values from 0 to 999, as said below
Outputs:
- updated: float32 [7168, 7168], P('row', 'col')
Inputs may be any that keep to these rules, and one draw needn't show every extreme that they name: amplitudes is exactly symmetric. integrals is exactly symmetric. pair_occ[p] mod 8 equals pair_vir[p] mod 8 (one irrep block), and no pair (pair_occ[p], pair_vir[p]) occurs twice. `pair_vir`: see pair_occ.
All inputs are finite; a program needn't handle non-finite values.
Results may differ from a plain program's by a relative error of at most 0.0003.
Values may be sent and summed in bfloat16 or wider, within the bound.
No kernel may reach another device: no remote copies, remote signals or barrier semaphores. Data moves between devices by JAX's collectives and lax.ppermute only.
A program may use at most 128 MiB of HBM per device.

v0:
```python
import jax
import jax.numpy as jnp
from jax import lax
from jax.sharding import PartitionSpec as P


def lookup(energies, orbital_index):
    labels = jnp.arange(energies.shape[0], dtype=jnp.int32)
    picked = jnp.where(orbital_index[:, None] == labels[None, :], energies[None, :], 0.0)
    return jnp.sum(picked, axis=1)


def shards(amplitudes, integrals, occ_energy, vir_energy, pair_occ, pair_vir):
    tile_rows, tile_cols = amplitudes.shape
    left_local = jnp.stack((amplitudes, integrals))
    right_local = jnp.stack((integrals, amplitudes))
    row_panels = lax.all_gather(left_local, "col", axis=2, tiled=True)
    summed = jnp.einsum(
        "lrk,lkc->rc",
        row_panels,
        lax.all_gather(right_local, "row", axis=1, tiled=True),
        preferred_element_type=jnp.float32,
    )
    row_start = lax.axis_index("row") * tile_rows
    col_start = lax.axis_index("col") * tile_cols
    row_occ = lax.dynamic_slice_in_dim(pair_occ, row_start, tile_rows)
    row_vir = lax.dynamic_slice_in_dim(pair_vir, row_start, tile_rows)
    col_occ = lax.dynamic_slice_in_dim(pair_occ, col_start, tile_cols)
    col_vir = lax.dynamic_slice_in_dim(pair_vir, col_start, tile_cols)
    row_gap = lookup(occ_energy, row_occ) - lookup(vir_energy, row_vir)
    col_gap = lookup(occ_energy, col_occ) - lookup(vir_energy, col_vir)
    return summed / (row_gap[:, None] + col_gap[None, :])


def solution(mesh):
    return jax.shard_map(
        shards,
        mesh=mesh,
        in_specs=(P("row", "col"), P("row", "col"), P(), P(), P(), P()),
        out_specs=P("row", "col"),
        check_vma=False,
    )
```

profile of v0, /device:TPU:1, one launch (start us, length us, event | category | flops | bytes accessed | tf_op | source)
XLA Modules:
  0.0 323.7 jit_solution(3779648207988396233)
XLA Ops:
  6.5 0.0 all-gather.3.cloned.1.call-start
  6.5 4.0 %pad_maximum_fusion.1 = (bf16[2,448,896]{2,1,0:T(8,128)(2,1)}, bf16[2,448,896]{2,1,0:T(8,128)(2,1)}) fusion(bf16[1,448,896]{2,1,0:T(8,128)(2,1)} %bitcast.6, bf16[1,448,896]{2,1,0:T(8,128)(2,1)} %bitcast.7), kind=kLoop, calls=%fused_computation.5 | loop fusion | flops 1605632 | bytes 4816896 | tf_op jit(solution)/shard_map/stack | solution.py:16
  10.5 0.0 copy-start.1
  10.5 0.0 copy-start
  10.5 0.0 all-gather.3.cloned.1.call-update
  10.5 0.0 all-gather.5.cloned.1.call-start
  10.6 0.7 all-gather.5.cloned.1.call-update
  11.3 0.8 dynamic_slice.14
  12.1 0.8 dynamic_slice.15
  12.9 0.8 dynamic_slice.12
  13.6 0.8 dynamic_slice.13
  14.4 0.0 copy-done.1
  14.4 0.1 select_reduce_fusion.2
  14.5 0.0 copy-done
  14.5 0.5 select_reduce_fusion
  15.0 0.1 select_reduce_fusion.3
  15.1 0.3 select_reduce_fusion.1
  15.5 146.1 %all-gather.3.cloned.1.call-done = bf16[2,448,7168]{2,1,0:T(8,128)(2,1)} async-done(((bf16[2,448,896]{2,1,0:T(8,128)(2,1)}), bf16[2,448,7168]{2,1,0:T(8,128)(2,1)}) %all-gather.3.cloned.1.call-update) | async-done | bytes 12845072 | tf_op jit(solution)/shard_map/all_gather | solution.py:17
  161.6 133.8 %all-gather.5.cloned.1.call-done = bf16[2,7168,896]{2,1,0:T(8,128)(2,1)} async-done(((bf16[2,448,896]{2,1,0:T(8,128)(2,1)}), bf16[2,7168,896]{2,1,0:T(8,128)(2,1)}) %all-gather.5.cloned.1.call-update) | async-done | bytes 25690128 | tf_op jit(solution)/shard_map/all_gather | solution.py:21
  295.4 21.5 %bitcast_divide_fusion = f32[448,896]{1,0:T(8,128)} fusion(bf16[2,448,7168]{2,1,0:T(8,128)(2,1)} %all-gather.3.cloned.1.call-done, bf16[2,7168,896]{2,1,0:T(8,128)(2,1)} %all-gather.5.cloned.1.call-done, f32[896]{0:T(1024)S(1)} %sub.15, f32[448]{0:T(512)S(1)} %sub.14), kind=kOutput, calls=%fused_computation.6 | convolution fusion | flops 11509972992 | bytes 40146176 | tf_op jit(solution)/shard_map/lrk,lkc->rc/dot_general | solution.py:18
  (2 shorter events, 0.0 us)
Async XLA Ops:
  6.5 155.0 %all-gather.3.cloned.1.call-start = ((), (), s32[]{:S(2)}) async-start(), calls=%async_computation | async-start | bytes 14450688 | tf_op jit(solution)/shard_map/all_gather | solution.py:17
  10.5 3.9 %copy-start.1 = (f32[80]{0:T(128)S(1)}, f32[80]{0:T(128)}, u32[]{:S(2)}) copy-start(f32[80]{0:T(128)} %param.8) | copy-start | bytes 964
  10.5 4.0 %copy-start = (f32[1000]{0:T(1024)S(1)}, f32[1000]{0:T(1024)}, u32[]{:S(2)}) copy-start(f32[1000]{0:T(1024)} %param.9) | copy-start | bytes 12004
  10.5 284.8 %all-gather.5.cloned.1.call-start = ((), (), s32[]{:S(2)}) async-start(), calls=%async_computation.1 | async-start | bytes 27295744 | tf_op jit(solution)/shard_map/all_gather | solution.py:21
Sparse Core Ops, SparseCore 0:
  10.7 150.8 all-gather.2
  163.2 132.1 all-gather.4
where the time goes:
time: 324 us
  waiting for transfers between devices  281 us (87%)
  matrix products  21.5 us (7%)
  between operations  13.4 us (4%)
  other arithmetic  5.01 us (2%)
    all_gather x1, waiting for transfers between devices, shards(): row_panels = lax.all_gather(left_local, 'col', axis=2, tiled=True)  146 us
    all_gather x1, waiting for transfers between devices, shards(): lax.all_gather(right_local, 'row', axis=1, tiled=True)  134 us
    dot_general x1, matrix products, shards(): jnp.einsum('lrk,lkc->rc', row_panels, lax.all_gather(right_local, 'row',...  21.5 us
  transfers between devices with their start and end apart: 2, of which 2 were waited for; matrix products, arithmetic and copies ran while one was open for 1% of the time, Pallas kernels for 0%

commit v1 on v0

--- a/solution.py
+++ b/solution.py
@@ -18,7 +18,9 @@
     summed = jnp.einsum(
         "lrk,lkc->rc",
         row_panels,
-        lax.all_gather(right_local, "row", axis=1, tiled=True),
+        jnp.concatenate(
+            lax.all_to_all(jnp.stack([right_local] * lax.axis_size("row")), "row", 0, 0), axis=1
+        ),
         preferred_element_type=jnp.float32,
     )
     row_start = lax.axis_index("row") * tile_rows

time: 324 us -> 445 us (1.37)
  waiting for transfers between devices: 281 us -> 365 us
  local copies, waits for them, and re-layouts: 3.1 us -> 32.6 us
  starting transfers between devices: 0.04 us -> 7.34 us
    all_to_all x0 -> x1, waiting for transfers between devices: none -> 340 us  [shards(): lax.all_to_all(jnp.stack([right_local] * lax.axis_size('row')), 'row', 0, 0)]
    all_gather x1 -> x0, waiting for transfers between devices: 134 us -> none  [shards(): lax.all_gather(right_local, 'row', axis=1, tiled=True)]
    all_gather x1, waiting for transfers between devices: 146 us -> 24.5 us  [shards(): row_panels = lax.all_gather(left_local, 'col', axis=2, tiled=True)]
    reshape x0 -> x1, local copies, waits for them, and re-layouts: none -> 21 us  [shards(): jnp.concatenate(lax.all_to_all(jnp.stack([right_local] * lax.axis_size('r...]
    another operation x0 -> x1, local copies, waits for them, and re-layouts: none -> 8.56 us  [shards(): jnp.stack([right_local] * lax.axis_size('row'))]
    all_to_all x0 -> x1, starting transfers between devices: none -> 7.3 us  [shards(): lax.all_to_all(jnp.stack([right_local] * lax.axis_size('row')), 'row', 0, 0)]
  transfers between devices with their start and end apart: 2 -> 2, of which waited for: 2 -> 2; matrix products, arithmetic and copies ran while one was open for 1% -> 6% of each run, Pallas kernels for 0% -> 0%
where the time goes in v1:
time: 445 us; the launch traced here: 444 us
  waiting for transfers between devices  365 us (82%)
  local copies, waits for them, and re-layouts  32.6 us (7%)
  matrix products  21.6 us (5%)
  between operations  13.4 us (3%)
  starting transfers between devices  7.34 us (2%)
    all_to_all x1, waiting for transfers between devices, shards(): lax.all_to_all(jnp.stack([right_local] * lax.axis_size('row')), 'row', 0, 0)  340 us
    all_gather x1, waiting for transfers between devices, shards(): row_panels = lax.all_gather(left_local, 'col', axis=2, tiled=True)  24.5 us
    dot_general x1, matrix products, shards(): jnp.einsum('lrk,lkc->rc', row_panels, jnp.concatenate(lax.all_to_all(jnp....  21.6 us
    reshape x1, local copies, waits for them, and re-layouts, shards(): jnp.concatenate(lax.all_to_all(jnp.stack([right_local] * lax.axis_size('r...  21 us
  transfers between devices with their start and end apart: 2, of which 2 were waited for; matrix products, arithmetic and copies ran while one was open for 6% of the time, Pallas kernels for 0%

profile of v1, /device:TPU:1, one launch (start us, length us, event | category | flops | bytes accessed | tf_op | source)
XLA Modules:
  0.0 444.4 jit_solution(6157308351587136310)
XLA Ops:
  6.5 3.4 pad_maximum_fusion.1
  9.9 8.6 %stack.14 = bf16[16,2,448,896]{3,2,1,0:T(8,128)(2,1)} broadcast(bf16[2,448,896]{2,1,0:T(8,128)(2,1)S(1)} %get-tuple-element.5), dimensions={1,2,3} | broadcast | bytes 27295744 | tf_op jit(solution)/shard_map/stack | solution.py:22
  18.5 0.0 copy-start.1
  18.5 0.0 copy-start
  18.5 7.3 %all-to-all-start = ((bf16[16,2,448,896]{3,2,1,0:T(8,128)(2,1)}), bf16[16,2,448,896]{3,2,1,0:T(8,128)(2,1)}, u32[]{:S(2)}, u32[]{:S(2)}) async-start(bf16[16,2,448,896]{3,2,1,0:T(8,128)(2,1)} %stack.14), calls=%async_computation | async-start | bytes 51380224 | tf_op jit(solution)/shard_map/all_to_all | solution.py:22
  25.8 0.0 all-gather.2.cloned.1.call-start
  25.9 0.7 all-gather.2.cloned.1.call-update
  26.6 0.8 dynamic_slice.15
  27.3 0.8 dynamic_slice.14
  28.1 0.8 dynamic_slice.13
  28.9 0.8 dynamic_slice.12
  29.6 0.0 copy-done.1
  29.6 0.1 select_reduce_fusion.2
  29.8 0.0 copy-done
  29.8 0.5 select_reduce_fusion
  30.3 0.1 select_reduce_fusion.3
  30.4 0.3 select_reduce_fusion.1
  30.7 339.7 %all-to-all-done = bf16[16,2,448,896]{3,2,1,0:T(8,128)(2,1)} async-done(((bf16[16,2,448,896]{3,2,1,0:T(8,128)(2,1)}), bf16[16,2,448,896]{3,2,1,0:T(8,128)(2,1)}, u32[]{:S(2)}, u32[]{:S(2)}) %all-to-all-start) | async-done | bytes 25690144 | tf_op jit(solution)/shard_map/all_to_all | solution.py:22
  370.4 21.0 %copy.8 = bf16[2,16,448,896]{3,2,1,0:T(8,128)(2,1)} copy(bf16[2,16,448,896]{3,2,0,1:T(8,128)(2,1)} %bitcast.2) | data formatting | bytes 51380224 | tf_op jit(solution)/shard_map/reshape | solution.py:21
  391.4 24.5 %all-gather.2.cloned.1.call-done = bf16[2,448,7168]{2,1,0:T(8,128)(2,1)} async-done(((bf16[2,448,896]{2,1,0:T(8,128)(2,1)}), bf16[2,448,7168]{2,1,0:T(8,128)(2,1)}) %all-gather.2.cloned.1.call-update) | async-done | bytes 12845072 | tf_op jit(solution)/shard_map/all_gather | solution.py:17
  415.9 21.6 %bitcast_divide_fusion = f32[448,896]{1,0:T(8,128)} fusion(bf16[2,448,7168]{2,1,0:T(8,128)(2,1)} %all-gather.2.cloned.1.call-done, bf16[2,7168,896]{2,1,0:T(8,128)(2,1)} %bitcast.8, f32[896]{0:T(1024)S(1)} %sub.15, f32[448]{0:T(512)S(1)} %sub.14), kind=kOutput, calls=%fused_computation.6 | convolution fusion | flops 11509972992 | bytes 40146176 | tf_op jit(solution)/shard_map/lrk,lkc->rc/dot_general | solution.py:18
  (2 shorter events, 0.0 us)
Async XLA Ops:
  18.5 11.1 %copy-start.1 = (f32[80]{0:T(128)S(1)}, f32[80]{0:T(128)}, u32[]{:S(2)}) copy-start(f32[80]{0:T(128)} %param.8) | copy-start | bytes 964
  18.5 11.3 %copy-start = (f32[1000]{0:T(1024)S(1)}, f32[1000]{0:T(1024)}, u32[]{:S(2)}) copy-start(f32[1000]{0:T(1024)} %param.9) | copy-start | bytes 12004
  18.5 351.9 %all-to-all-start = ((bf16[16,2,448,896]{3,2,1,0:T(8,128)(2,1)}), bf16[16,2,448,896]{3,2,1,0:T(8,128)(2,1)}, u32[]{:S(2)}, u32[]{:S(2)}) async-start(bf16[16,2,448,896]{3,2,1,0:T(8,128)(2,1)} %stack.14), calls=%async_computation | async-start | bytes 51380224 | tf_op jit(solution)/shard_map/all_to_all | solution.py:22
  25.8 390.1 %all-gather.2.cloned.1.call-start = ((), (), s32[]{:S(2)}) async-start(), calls=%async_computation.1 | async-start | bytes 14450688 | tf_op jit(solution)/shard_map/all_gather | solution.py:17
Sparse Core Ops, SparseCore 0:
  29.0 386.8 all-gather.1
